TPU v7x, 512 devices: a whole 4x8x8 slice. The times are simulated.
512 devices in a mesh: tile: 32 (over y, z_lo), pos: 16 (over x, z_hi, core).
Axes of the slice: x: 4, y: 8, z: 8 (z_hi: 2, z_lo: 4; z = z_hi * 4 + z_lo), core: 2. Of those that a mesh axis runs over, the one named last changes fastest.
Arguments:
- amplitude: float32 [32, 2, 256, 256], P('tile'), may hold values from 0.6 to 1
- phase_map: float32 [32, 2, 256, 256], P('tile'), may hold values from -3.140625 to 3.140625
- probe_modes: float32 [2, 3, 128, 128], replicated, may hold values from -4 to 4
- offsets: int32 [32, 32, 2], P('tile', 'pos'), may hold values from 0 to 128
- pos_counts: int32 [32, 16], P('tile', 'pos'), may hold values from 1 to 2, as said below
- measured: float32 [32, 32, 128, 128], P('tile', 'pos'), may hold values from 0.1 to 2
Outputs:
- updated_object: float32 [32, 2, 2, 256, 256], P('tile')
Inputs may be any that keep to these rules, and one draw needn't show every extreme that they name: The first pos_counts[t, p] slots of subset p of tile t hold positions; its other slots are padding and take no part. In every tile some subset has 2 live slots.
All inputs are finite; a program needn't handle non-finite values.
Results may differ from a plain program's by a relative error of at most 0.0015.
Values sent between devices are 32-bit elements; how exact they have to be, the bound alone decides.
A program may use at most 64 MiB of HBM per device.

v0:
```python
import math

import jax
import jax.numpy as jnp
from jax import lax
from jax.sharding import PartitionSpec as P

CORRELATION = 64
GRID_COLS = 4


step_size = 0.1
fresnel_rate = 0.0123


def padded(value, sides, width):
    for axis, dim in sides:
        count, length = (lax.axis_size(axis), value.shape[dim])
        up = [(i, (i + 1) % count) for i in range(count - 1)]
        down = [(j, i) for i, j in up]
        last = lax.slice_in_dim(value, length - width, length, axis=dim)
        initial = lax.slice_in_dim(value, 0, width, axis=dim)
        before = lax.ppermute(last, axis, up)
        after = lax.ppermute(initial, axis, down)
        value = jnp.concatenate([before, value, after], axis=dim)
    return value


def shifted(value, axis, steps):
    count = lax.axis_size(axis)
    initial, last = (max(0, -steps), min(count, count - steps))
    return lax.ppermute(value, axis, [(source, source + steps) for source in range(initial, last)])


def make_tables(extent):
    counter = jnp.arange(extent, dtype=jnp.int32)
    product = counter[:, None] * counter[None, :] % extent
    angles = product.astype(jnp.float32) * (2.0 * math.pi / extent)
    scaling = 1.0 / math.sqrt(extent)
    table_re = (jnp.cos(angles) * scaling).astype(jnp.bfloat16)
    table_im = (-jnp.sin(angles) * scaling).astype(jnp.bfloat16)
    centered = ((counter + extent // 2) % extent - extent // 2).astype(jnp.float32)
    phases = -fresnel_rate * (
        centered[:, None] * centered[:, None] + centered[None, :] * centered[None, :]
    )
    return (table_re, table_im, jnp.cos(phases), jnp.sin(phases))


def right_pass(wave_re, wave_im, table_re, table_im):
    extent = wave_re.shape[-1]
    stacked = jnp.concatenate([wave_re, wave_im], axis=0).astype(jnp.bfloat16).reshape(-1, extent)
    joined = jnp.concatenate([table_re, table_im], axis=1)
    result = jnp.dot(stacked, joined, preferred_element_type=jnp.float32)
    half_rows = result.shape[0] // 2
    upper_part = result[:half_rows]
    lower_part = result[half_rows:]
    out_re = upper_part[:, :extent] - lower_part[:, extent:]
    out_im = upper_part[:, extent:] + lower_part[:, :extent]
    return (out_re.reshape(wave_re.shape), out_im.reshape(wave_re.shape))


def transform(wave_re, wave_im, table_re, table_im):
    first_re, first_im = right_pass(wave_re, wave_im, table_re, table_im)
    second_re, second_im = right_pass(
        jnp.swapaxes(first_re, 1, 2), jnp.swapaxes(first_im, 1, 2), table_re, table_im
    )
    return (jnp.swapaxes(second_re, 1, 2), jnp.swapaxes(second_im, 1, 2))


def slot_loss(cropped, probe_modes, target, tables):
    table_re, table_im, kernel_re, kernel_im = tables
    wave_re = probe_modes[0] * cropped[0, 0] - probe_modes[1] * cropped[1, 0]
    wave_im = probe_modes[0] * cropped[1, 0] + probe_modes[1] * cropped[0, 0]
    spread_re, spread_im = transform(wave_re, wave_im, table_re, table_im)
    moved_re = spread_re * kernel_re - spread_im * kernel_im
    moved_im = spread_re * kernel_im + spread_im * kernel_re
    inverse_re, inverse_im = transform(moved_re, moved_im, table_re, -table_im)
    wave_re = inverse_re * cropped[0, 1] - inverse_im * cropped[1, 1]
    wave_im = inverse_re * cropped[1, 1] + inverse_im * cropped[0, 1]
    far_re, far_im = transform(wave_re, wave_im, table_re, table_im)
    intensity = jnp.sum(far_re * far_re + far_im * far_im, axis=0)
    misfit = intensity - target
    return 0.5 * jnp.sum(misfit * misfit)


def slot_gradient(cropped, probe_modes, target, tables):
    return jax.grad(slot_loss)(cropped, probe_modes, target, tables)


def local_gradient(current, probe_modes, selected, tables):
    window = probe_modes.shape[-1]
    layers = current.shape[1]
    anchor = jnp.zeros((), jnp.int32)
    accumulated = jnp.zeros_like(current)
    for offset_pair, is_live, target in selected:
        starts = (anchor, anchor, offset_pair[0], offset_pair[1])
        cropped = lax.dynamic_slice(current, starts, (2, layers, window, window))
        gradient = slot_gradient(cropped, probe_modes, target, tables) * is_live.astype(jnp.float32)
        region = lax.dynamic_slice(accumulated, starts, (2, layers, window, window))
        accumulated = lax.dynamic_update_slice(accumulated, region + gradient, starts)
    return accumulated


def add_strips(gradient, edge_rows):
    row_count = gradient.shape[-2]
    extent = gradient.shape[-1]
    widened = padded(gradient, (("tile", 3),), CORRELATION)
    from_above = shifted(gradient[:, :, row_count - edge_rows :, :], "tile", GRID_COLS)
    from_below = shifted(gradient[:, :, :edge_rows, :], "tile", -GRID_COLS)
    left_part = widened[..., :CORRELATION]
    right_part = widened[..., extent + CORRELATION :]
    result = gradient.at[..., :CORRELATION].add(left_part)
    result = result.at[..., extent - CORRELATION :].add(right_part)
    result = result.at[:, :, :edge_rows, :].add(from_above)
    result = result.at[:, :, row_count - edge_rows :, :].add(from_below)
    return result


def per_device(amplitude, phase_map, probe_modes, offsets, pos_counts, measured):
    tables = make_tables(measured.shape[-1])
    current = jnp.stack(
        [amplitude[0] * jnp.cos(phase_map[0]), amplitude[0] * jnp.sin(phase_map[0])], axis=0
    )
    slot_count = offsets.shape[1]
    selected = []
    for slot_index in range(slot_count):
        selected.append(
            (offsets[0, slot_index], slot_index < pos_counts[0, 0], measured[0, slot_index])
        )
    partial_value = local_gradient(current, probe_modes, selected, tables)
    summed = lax.psum(partial_value, "pos")
    current = current - step_size * add_strips(summed, CORRELATION)
    return current[None]


def solution(mesh):
    in_specs = (
        P("tile", None, None, None),
        P("tile", None, None, None),
        P(),
        P("tile", "pos", None),
        P("tile", "pos"),
        P("tile", "pos", None, None),
    )
    out_specs = P("tile", None, None, None, None)
    return jax.shard_map(
        per_device, mesh=mesh, in_specs=in_specs, out_specs=out_specs, check_vma=False
    )
```

profile of v0, /device:TPU:1, one launch (start us, length us, event | category | flops | bytes accessed | tf_op | source)
XLA Modules:
  0.0 297.5 jit_solution(12579524430803322148)
XLA Ops:
  6.5 1.4 fusion.166
  13.1 0.3 multiply_convert_fusion
  13.4 0.3 fusion.120
  16.3 2.9 cosine_multiply_fusion
  19.5 0.6 slice_bitcast_fusion.1
  20.1 0.4 copy-done.2
  21.7 0.3 fusion.116
  23.6 0.7 fusion.61
  24.5 0.8 copy-done.7
  25.7 0.8 copy-done.18
  26.5 0.6 fusion.165
  27.2 0.9 copy.153
  28.1 0.6 reduce_sum.163
  28.8 0.8 fusion.114
  30.4 0.3 fusion.10
  30.7 0.8 fusion.84
  33.9 0.8 add_bitcast_fusion.5
  35.1 0.3 fusion.7
  35.7 0.3 fusion.6
  36.0 0.8 copy-done.5
  38.1 0.7 copy-done.3
  39.1 0.7 fusion.55
  39.9 0.8 copy-done.8
  41.2 0.6 reduce_sum.182
  41.8 1.0 copy.154
  43.9 0.8 copy-done.4
  44.7 0.8 fusion.72
  45.8 0.3 fusion.3
  46.4 0.3 fusion.2
  47.8 0.3 fusion
  48.9 0.6 copy-done.14
  49.9 3.4 %dynamic_update_slice.6 = f32[2,2,256,256]{3,2,1,0:T(8,128)S(1)} dynamic-update-slice(f32[2,2,256,256]{3,2,1,0:T(8,128)S(1)} %broadcast_in_dim.84, f32[2,2,128,128]{3,2,1,0:T(8,128)S(1)} %add_multiply_fusion, s32[]{:T(128)} %constant.141.clone.1, s32[]{:T(128)} %constant.141.clone.1, s32[]{:T(128)S(6)} %select_n.75, s32[]{:T(128)S(6)} %select_n.76) | dynamic-update-slice | bytes 524292 | tf_op jit(solution)/shard_map/dynamic_update_slice | solution.py:100
  53.4 3.4 %dynamic_update_slice.7 = f32[2,2,256,256]{3,2,1,0:T(8,128)S(1)} dynamic-update-slice(f32[2,2,256,256]{3,2,1,0:T(8,128)S(1)} %dynamic_update_slice.6, f32[2,2,128,128]{3,2,1,0:T(8,128)S(1)} %multiply_add_fusion, s32[]{:T(128)} %constant.141.clone.1, s32[]{:T(128)} %constant.141.clone.1, s32[]{:T(128)S(6)} %select_n.79, s32[]{:T(128)S(6)} %select_n.80) | dynamic-update-slice | bytes 524292 | tf_op jit(solution)/shard_map/dynamic_update_slice | solution.py:100
  56.8 1.0 copy-done.1
  57.8 193.3 %all-reduce.90.cloned.1.call-done = f32[2,2,256,256]{3,2,1,0:T(8,128)} async-done(((f32[2,2,256,256]{3,2,1,0:T(8,128)}), f32[2,2,256,256]{3,2,1,0:T(8,128)}) %all-reduce.90.cloned.1.call-update) | async-done | bytes 1048592 | tf_op jit(solution)/shard_map/psum | solution.py:131
  251.1 1.3 slice.566
  252.4 2.4 collective-permute-start
  254.9 9.6 %collective-permute-done = f32[2,2,256,64]{3,2,1,0:T(8,128)S(1)} collective-permute-done((f32[2,2,256,64]{3,2,1,0:T(8,128)S(1)}, f32[2,2,256,64]{3,2,1,0:T(8,128)S(1)}, u32[]{:S(2)}, u32[]{:S(2)}) %collective-permute-start) | collective-permute-done | bytes 262176 | tf_op jit(solution)/shard_map/ppermute | solution.py:23
  264.5 0.9 fusion.152
  265.4 1.3 collective-permute-start.1
  266.6 0.9 fusion.151
  267.5 9.4 %collective-permute-start.2 = (f32[2,2,64,256]{3,2,1,0:T(8,128)}, f32[2,2,64,256]{3,2,1,0:T(8,128)}, u32[]{:S(2)}, u32[]{:S(2)}) collective-permute-start(f32[2,2,64,256]{3,2,1,0:T(8,128)} %get-tuple-element.80), channel_id=1, source_target_pairs={{0,64},{16,80},{32,96},{48,112},{64,128},{80,144},{96,160},{112,17... | collective-permute-start | bytes 786440 | tf_op jit(solution)/shard_map/ppermute | solution.py:32
  276.9 1.3 collective-permute-start.3
  278.2 2.3 scatter-add.14
  280.7 2.4 scatter-add.15
  283.1 1.0 fusion.53
  284.1 5.4 %collective-permute-done.3 = f32[2,2,64,256]{3,2,1,0:T(8,128)S(1)} collective-permute-done((f32[2,2,64,256]{3,2,1,0:T(8,128)}, f32[2,2,64,256]{3,2,1,0:T(8,128)S(1)}, u32[]{:S(2)}, u32[]{:S(2)}) %collective-permute-start.3) | collective-permute-done | bytes 262176 | tf_op jit(solution)/shard_map/ppermute | solution.py:32
  289.6 1.1 fusion.13
  (163 shorter events, 12.9 us)
Async XLA Ops:
  6.5 244.6 %all-reduce.90.cloned.1.call-start = ((), (), s32[]{:S(2)}) async-start(), calls=%async_computation | async-start | bytes 2097152 | tf_op jit(solution)/shard_map/psum | solution.py:131
  19.4 1.0 copy-start.2
  24.3 0.9 copy-start.7
  25.6 0.9 copy-start.18
  36.0 0.9 copy-start.5
  36.0 0.9 copy-start.6
  37.9 0.8 copy-start.3
  39.8 0.9 copy-start.8
  41.8 1.0 copy-start.13
  43.8 0.8 copy-start.4
  48.8 0.8 copy-start.14
  48.8 0.9 copy-start.15
  48.8 0.9 copy-start.16
  48.8 0.9 copy-start.17
  49.8 3.4 %copy-start.9 = (f32[128,128]{1,0:T(8,128)S(1)}, f32[128,128]{1,0:T(8,128)}, u32[]{:S(2)}) copy-start(f32[128,128]{1,0:T(8,128)} %get-tuple-element.67) | copy-start | bytes 196612
  49.8 3.4 %copy-start.10 = (f32[128,128]{1,0:T(8,128)S(1)}, f32[128,128]{1,0:T(8,128)}, u32[]{:S(2)}) copy-start(f32[128,128]{1,0:T(8,128)} %get-tuple-element.68) | copy-start | bytes 196612
  49.8 3.4 %copy-start.11 = (f32[128,128]{1,0:T(8,128)S(1)}, f32[128,128]{1,0:T(8,128)}, u32[]{:S(2)}) copy-start(f32[128,128]{1,0:T(8,128)} %get-tuple-element.69) | copy-start | bytes 196612
  49.8 3.4 %copy-start.12 = (f32[128,128]{1,0:T(8,128)S(1)}, f32[128,128]{1,0:T(8,128)}, u32[]{:S(2)}) copy-start(f32[128,128]{1,0:T(8,128)} %get-tuple-element.70) | copy-start | bytes 196612
  56.8 1.0 copy-start.1
  251.1 13.4 %copy-start = (f32[2,2,256,256]{3,2,1,0:T(8,128)S(1)}, f32[2,2,256,256]{3,2,1,0:T(8,128)}, u32[]{:S(2)}) copy-start(f32[2,2,256,256]{3,2,1,0:T(8,128)} %all-reduce.90.cloned.1.call-done) | copy-start | bytes 3145732
  252.4 12.0 %collective-permute-start = (f32[2,2,256,64]{3,2,1,0:T(8,128)S(1)}, f32[2,2,256,64]{3,2,1,0:T(8,128)S(1)}, u32[]{:S(2)}, u32[]{:S(2)}) collective-permute-start(f32[2,2,256,64]{3,2,1,0:T(8,128)S(1)} %slice.566), channel_id=1, source_target_pairs={{0,16},{16,32},{32,48},{48,64},{64,80},{80,96},{96,112},{112,128},... | collective-permute-start | bytes 786440 | tf_op jit(solution)/shard_map/ppermute | solution.py:23
  265.4 15.1 %collective-permute-start.1 = (f32[2,2,256,64]{3,2,1,0:T(8,128)}, f32[2,2,256,64]{3,2,1,0:T(8,128)S(1)}, u32[]{:S(2)}, u32[]{:S(2)}) collective-permute-start(f32[2,2,256,64]{3,2,1,0:T(8,128)} %get-tuple-element.81), channel_id=1, source_target_pairs={{16,0},{32,16},{48,32},{64,48},{80,64},{96,80},{112,96},{128,112},... | collective-permute-start | bytes 786440 | tf_op jit(solution)/shard_map/ppermute | solution.py:24
  267.5 15.6 %collective-permute-start.2 = (f32[2,2,64,256]{3,2,1,0:T(8,128)}, f32[2,2,64,256]{3,2,1,0:T(8,128)}, u32[]{:S(2)}, u32[]{:S(2)}) collective-permute-start(f32[2,2,64,256]{3,2,1,0:T(8,128)} %get-tuple-element.80), channel_id=1, source_target_pairs={{0,64},{16,80},{32,96},{48,112},{64,128},{80,144},{96,160},{112,17... | collective-permute-start | bytes 786440 | tf_op jit(solution)/shard_map/ppermute | solution.py:32
  276.9 12.6 %collective-permute-start.3 = (f32[2,2,64,256]{3,2,1,0:T(8,128)}, f32[2,2,64,256]{3,2,1,0:T(8,128)S(1)}, u32[]{:S(2)}, u32[]{:S(2)}) collective-permute-start(f32[2,2,64,256]{3,2,1,0:T(8,128)} %get-tuple-element.79), channel_id=1, source_target_pairs={{64,0},{80,16},{96,32},{112,48},{128,64},{144,80},{160,96},{176,11... | collective-permute-start | bytes 786440 | tf_op jit(solution)/shard_map/ppermute | solution.py:32
Sparse Core Ops, SparseCore 0:
  57.9 193.1 all-reduce.89
where the time goes:
time: 302 us; the launch traced here: 298 us
  waiting for transfers between devices  208 us (69%)
  local copies, waits for them, and re-layouts  30.6 us (10%)
  between operations  22.9 us (8%)
  other arithmetic  15.4 us (5%)
  starting transfers between devices  14.4 us (5%)
  matrix products  5.87 us (2%)
    psum x1, waiting for transfers between devices, per_device(): summed = lax.psum(partial_value, 'pos')  193 us
    ppermute x2, starting transfers between devices, shifted(): lax.ppermute(value, axis, [(source, source + steps) for source in range(i...  10.7 us
    ppermute x1, waiting for transfers between devices, padded(): before = lax.ppermute(last, axis, up)  9.59 us
    unnamed x40, local copies, waits for them, and re-layouts  8.78 us
    dynamic_update_slice x2, local copies, waits for them, and re-layouts, local_gradient(): lax.dynamic_update_slice(accumulated, region + gradient, starts)  6.76 us
  transfers between devices with their start and end apart: 5, of which 3 were waited for; matrix products, arithmetic and copies ran while one was open for 2% of the time, Pallas kernels for 0%

commit v1 on v0

v1 whole, which is shorter than its diff:
```python
import functools
import math

import jax
import jax.numpy as jnp
import numpy as np
from jax import lax
from jax.experimental import pallas as pl
from jax.experimental.pallas import tpu as pltpu
from jax.sharding import PartitionSpec as P

MESH = pl.DeviceIdType.MESH
TILE = 256
WIN = 128
EDGE = 64
MODES = 3
LAYERS = 2
SLOTS = 2
SPAN = WIN + 8
STEP = 0.1
FRESNEL = 0.0123
SIN = (0.9999999957326958, -0.16666657991741893, 0.008333051059307331, -0.0001980907498047039, 2.605224199925007e-06)
COS = (0.9999999997806426, -0.49999999358456015, 0.04166663625748454, -0.001388836139270363, 2.476016095941152e-05, -2.6051488147238807e-07)


def make_tables():
    counter = np.arange(WIN)
    angles = (np.outer(counter, counter) % WIN).astype(np.float32) * np.float32(2.0 * math.pi / WIN)
    scaling = np.float32(1.0 / math.sqrt(WIN))
    f_re = (np.cos(angles) * scaling).astype(jnp.bfloat16)
    f_im = (-np.sin(angles) * scaling).astype(jnp.bfloat16)
    forward = np.block([[f_re, f_im], [-f_im, f_re]])
    inverse = np.block([[f_re, -f_im], [f_im, f_re]])
    centered = ((counter + WIN // 2) % WIN - WIN // 2).astype(np.float32)
    square = centered * centered
    phases = np.float32(-FRESNEL) * (square[:, None] + square[None, :])
    kernel = np.stack([np.cos(phases), np.sin(phases)]).astype(np.float32)
    return np.stack([forward, inverse]).astype(jnp.bfloat16), kernel


def horner(terms, u):
    total = jnp.full_like(u, terms[-1])
    for term in terms[-2::-1]:
        total = total * u + term
    return total


def polar(amplitude, phase):
    half = phase * 0.5
    u = half * half
    sine = half * horner(SIN, u)
    cosine = horner(COS, u)
    return amplitude - (2.0 * amplitude) * (sine * sine), (2.0 * amplitude) * (sine * cosine)


def times(a, b):
    return a[0] * b[0] - a[1] * b[1], a[0] * b[1] + a[1] * b[0]


def times_conj(a, b):
    return a[0] * b[0] + a[1] * b[1], a[1] * b[0] - a[0] * b[1]


def right_pass(waves, table):
    rows = [jnp.concatenate([re.astype(jnp.bfloat16), im.astype(jnp.bfloat16)], axis=1) for re, im in waves]
    result = jnp.dot(jnp.concatenate(rows, axis=0), table, preferred_element_type=jnp.float32)
    return [(result[i * WIN : (i + 1) * WIN, :WIN], result[i * WIN : (i + 1) * WIN, WIN:]) for i in range(len(waves))]


def left_pass(waves, table):
    columns = [jnp.concatenate([re.astype(jnp.bfloat16), im.astype(jnp.bfloat16)], axis=0) for re, im in waves]
    result = jnp.dot(table, jnp.concatenate(columns, axis=1), preferred_element_type=jnp.float32)
    return [(result[:WIN, i * WIN : (i + 1) * WIN], result[WIN:, i * WIN : (i + 1) * WIN]) for i in range(len(waves))]


def transform(waves, right, left):
    return left_pass(right_pass(waves, right), left)


def transform_back(waves, right, left):
    return right_pass(left_pass(waves, left), right)


def crop(ref, layer, base, shift, column):
    rows = ref[layer, pl.ds(base, SPAN), :]
    rows = pltpu.roll(rows, lax.rem(TILE - column, TILE), 1)[:, :WIN]
    return pltpu.roll(rows, lax.rem(SPAN - shift, SPAN), 0)[:WIN]


def spread_out(value, shift, column):
    tall = jnp.concatenate([value, jnp.zeros((SPAN - WIN, WIN), value.dtype)], axis=0)
    tall = pltpu.roll(tall, shift, 0)
    return pltpu.roll(jnp.concatenate([tall, jnp.zeros_like(tall)], axis=1), column, 1)


def add_all(values):
    total = values[0]
    for value in values[1:]:
        total = total + value
    return total


def slot_gradient(layers, probe_ref, target, tables_ref, kernel_ref):
    forward, inverse = tables_ref[0], tables_ref[1]
    kernel = (kernel_ref[0], kernel_ref[1])
    probes = [(probe_ref[0, m], probe_ref[1, m]) for m in range(MODES)]
    waves = [times(probe, layers[0]) for probe in probes]
    spread = transform(waves, forward, inverse)
    moved = [times(wave, kernel) for wave in spread]
    returned = transform(moved, inverse, forward)
    waves = [times(wave, layers[1]) for wave in returned]
    far = transform(waves, forward, inverse)
    misfit = add_all([re * re + im * im for re, im in far]) - target
    twice = misfit + misfit
    grads = transform_back([(twice * re, twice * im) for re, im in far], inverse, forward)
    second = [times_conj(grad, wave) for grad, wave in zip(grads, returned)]
    second = (add_all([v[0] for v in second]), add_all([v[1] for v in second]))
    grads = transform_back([times_conj(grad, layers[1]) for grad in grads], forward, inverse)
    grads = transform_back([times_conj(grad, kernel) for grad in grads], inverse, forward)
    first = [times_conj(grad, probe) for grad, probe in zip(grads, probes)]
    first = (add_all([v[0] for v in first]), add_all([v[1] for v in first]))
    return first, second


def gradient_kernel(off_ref, count_ref, amp_ref, phase_ref, probe_ref, measured_ref, tables_ref, kernel_ref, out_ref):
    out_ref[...] = jnp.zeros_like(out_ref)
    for slot in range(SLOTS):
        row, column = off_ref[slot, 0], off_ref[slot, 1]
        base = pl.multiple_of(jnp.minimum(row // 8 * 8, TILE - SPAN), 8)
        shift = row - base
        live = slot < count_ref[0, 0]
        layers = [
            polar(crop(amp_ref, layer, base, shift, column), crop(phase_ref, layer, base, shift, column))
            for layer in range(LAYERS)
        ]
        grads = slot_gradient(layers, probe_ref, measured_ref[slot], tables_ref, kernel_ref)
        for layer in range(LAYERS):
            for part in range(2):
                value = jnp.where(live, grads[layer][part], 0.0)
                out_ref[2 * part + layer, pl.ds(base, SPAN), :] += spread_out(value, shift, column)


def combine_kernel(
    part_ref, amp_ref, phase_ref, out_ref,
    pair, half, relay, merged, direct, final, block, zin, strips, strips_in, rows_in, send, recv,
):
    tile, pos = lax.axis_index("tile"), lax.axis_index("pos")
    tiles = lax.axis_size("tile")
    core, z_hi, x = lax.rem(pos, 2), lax.rem(pos // 2, 2), pos // 4
    z_lo = lax.rem(tile, 4)
    xo, xp, xm = lax.rem(x + 2, 4), lax.rem(x + 1, 4), lax.rem(x + 3, 4)

    def place(x_, z_, core_):
        return x_ * 4 + z_ * 2 + core_

    here = tile
    sibling = {"tile": here, "pos": place(x, z_hi, 1 - core)}
    right_x = {"tile": here, "pos": place(xp, z_hi, core)}
    left_x = {"tile": here, "pos": place(xm, z_hi, core)}
    across = {"tile": here, "pos": place(x, 1 - z_hi, core)}
    after_z = jnp.where(z_lo == 3, 1 - z_hi, z_hi)
    before_z = jnp.where(z_lo == 0, 1 - z_hi, z_hi)
    after = {"tile": lax.rem(tile + 1, tiles), "pos": place(x, after_z, core)}
    before = {"tile": lax.rem(tile + tiles - 1, tiles), "pos": place(x, before_z, core)}
    vertical = {"tile": lax.rem(tile + tiles + jnp.where(core == 0, -4, 4), tiles), "pos": place(x, z_hi, 1 - core)}

    partners = (sibling, right_x, left_x, across, after, before, vertical)
    barrier = pltpu.get_barrier_semaphore()
    for partner in partners:
        pl.semaphore_signal(barrier, inc=1, device_id=partner, device_id_type=MESH)
    pl.semaphore_wait(barrier, len(partners))

    started = []

    def push(index, src, dst, device):
        copy = pltpu.make_async_remote_copy(
            src_ref=src, dst_ref=dst, send_sem=send.at[index], recv_sem=recv.at[index],
            device_id=device, device_id_type=MESH,
        )
        copy.start()
        started.append(copy)
        return copy

    mine = pl.ds(pl.multiple_of(core * WIN, WIN), WIN)
    other = pl.ds(pl.multiple_of((1 - core) * WIN, WIN), WIN)
    upper, lower = pl.ds(0, EDGE), pl.ds(EDGE, EDGE)

    order = (xo, xp, xm, x)
    swaps = [push(k, part_ref.at[order[k], other], pair.at[k], sibling) for k in range(4)]

    def reduce_pair(k):
        swaps[k].wait_recv()
        half[k] = part_ref[order[k], mine, :] + pair[k]

    reduce_pair(0)
    to_right = push(4, half.at[0, upper], relay.at[0], right_x)
    to_left = push(5, half.at[0, lower], relay.at[1], left_x)
    reduce_pair(1)
    direct_right = push(6, half.at[1, lower], direct.at[1], right_x)
    reduce_pair(2)
    direct_left = push(7, half.at[2, upper], direct.at[0], left_x)
    reduce_pair(3)
    to_right.wait_recv()
    merged[0] = relay[0] + half[1, 0:EDGE, :]
    last_right = push(8, merged.at[0], final.at[0], right_x)
    to_left.wait_recv()
    merged[1] = relay[1] + half[2, EDGE:WIN, :]
    last_left = push(9, merged.at[1], final.at[1], left_x)
    direct_left.wait_recv()
    last_right.wait_recv()
    block[0:EDGE, :] = half[3, 0:EDGE, :] + (direct[0] + final[0])
    direct_right.wait_recv()
    last_left.wait_recv()
    block[EDGE:WIN, :] = half[3, EDGE:WIN, :] + (direct[1] + final[1])

    swap_z = push(10, block, zin, across)
    swap_z.wait()
    block[...] = block[...] + zin[...]

    edge_rows = pl.ds(pl.multiple_of(core * EDGE, EDGE), EDGE)
    swap_rows = push(11, block.at[edge_rows], rows_in, vertical)
    lane = lax.broadcasted_iota(jnp.int32, (EDGE, WIN), 1)
    low = lane < EDGE
    strips[0] = jnp.where(low, pltpu.roll(block[0:EDGE, WIN:], EDGE, 1), block[EDGE:WIN, WIN:])
    strips[1] = jnp.where(low, block[0:EDGE, :WIN], pltpu.roll(block[EDGE:WIN, :WIN], EDGE, 1))
    swap_after = push(12, strips.at[0], strips_in.at[0], after)
    swap_before = push(13, strips.at[1], strips_in.at[1], before)

    layer, part = lax.rem(x, 2), x // 2
    base = polar(amp_ref[layer, mine, :], phase_ref[layer, mine, :])
    base = jnp.where(part == 0, base[0], base[1])

    swap_after.wait_recv()
    swap_before.wait_recv()
    from_left = jnp.where(tile > 0, strips_in[0], 0.0)
    from_right = jnp.where(tile < tiles - 1, strips_in[1], 0.0)
    left_top = jnp.where(low, from_left, 0.0)
    left_bottom = jnp.where(low, pltpu.roll(from_left, EDGE, 1), 0.0)
    right_top = jnp.where(low, 0.0, pltpu.roll(from_right, EDGE, 1))
    right_bottom = jnp.where(low, 0.0, from_right)
    sides = jnp.concatenate(
        [jnp.concatenate([left_top, right_top], axis=1), jnp.concatenate([left_bottom, right_bottom], axis=1)], axis=0
    )
    swap_rows.wait_recv()
    vertical_live = jnp.where(core == 0, tile >= 4, tile < tiles - 4)
    edge = jnp.where(vertical_live, rows_in[...], 0.0)
    top = jnp.where(core == 0, edge, 0.0)
    bottom = jnp.where(core == 0, 0.0, edge)
    combined = block[...] + sides + jnp.concatenate([top, bottom], axis=0)
    out_ref[x, mine, :] = base - STEP * combined

    top_rows = pl.ds(pl.multiple_of(core * WIN, EDGE), EDGE)
    bottom_rows = pl.ds(pl.multiple_of(core * WIN + EDGE, EDGE), EDGE)

    def share(index, plane, rows, device):
        return push(index, out_ref.at[plane, rows], out_ref.at[plane, rows], device)

    a_right = share(14, x, top_rows, right_x)
    b_left = share(15, x, bottom_rows, left_x)
    b_right = share(16, x, bottom_rows, right_x)
    a_left = share(17, x, top_rows, left_x)
    pairs = [share(18, x, mine, sibling)]
    a_right.wait_recv()
    a_next = share(19, xm, top_rows, right_x)
    b_left.wait_recv()
    b_next = share(20, xp, bottom_rows, left_x)
    b_right.wait_recv()
    pairs.append(share(21, xm, mine, sibling))
    a_left.wait_recv()
    pairs.append(share(22, xp, mine, sibling))
    a_next.wait_recv()
    b_next.wait_recv()
    pairs.append(share(23, xo, mine, sibling))
    for copy in pairs:
        copy.wait_recv()
    for copy in started:
        if copy is not swap_z:
            copy.wait_send()


def per_device(amplitude, phase_map, probe_modes, offsets, pos_counts, measured):
    tables, kernel = make_tables()
    vmem = pl.BlockSpec(memory_space=pltpu.VMEM)
    smem = pl.BlockSpec(memory_space=pltpu.SMEM)
    f32 = jnp.float32
    planes = jax.ShapeDtypeStruct((2 * LAYERS, TILE, TILE), f32)
    partial = pl.pallas_call(
        gradient_kernel,
        out_shape=planes,
        in_specs=[smem, smem] + [vmem] * 6,
        out_specs=vmem,
        name="gradient",
    )(offsets[0], pos_counts, amplitude[0], phase_map[0], probe_modes, measured[0], jnp.asarray(tables), jnp.asarray(kernel))
    updated = pl.pallas_call(
        combine_kernel,
        out_shape=planes,
        in_specs=[vmem] * 3,
        out_specs=vmem,
        scratch_shapes=[
            pltpu.VMEM((4, WIN, TILE), f32),
            pltpu.VMEM((4, WIN, TILE), f32),
            pltpu.VMEM((2, EDGE, TILE), f32),
            pltpu.VMEM((2, EDGE, TILE), f32),
            pltpu.VMEM((2, EDGE, TILE), f32),
            pltpu.VMEM((2, EDGE, TILE), f32),
            pltpu.VMEM((WIN, TILE), f32),
            pltpu.VMEM((WIN, TILE), f32),
            pltpu.VMEM((2, EDGE, WIN), f32),
            pltpu.VMEM((2, EDGE, WIN), f32),
            pltpu.VMEM((EDGE, TILE), f32),
            pltpu.SemaphoreType.DMA((24,)),
            pltpu.SemaphoreType.DMA((24,)),
        ],
        compiler_params=pltpu.CompilerParams(collective_id=0, has_side_effects=True),
        name="combine",
    )(partial, amplitude[0], phase_map[0])
    return updated.reshape(1, 2, LAYERS, TILE, TILE)


def solution(mesh):
    in_specs = (
        P("tile", None, None, None),
        P("tile", None, None, None),
        P(),
        P("tile", "pos", None),
        P("tile", "pos"),
        P("tile", "pos", None, None),
    )
    out_specs = P("tile", None, None, None, None)
    return jax.shard_map(per_device, mesh=mesh, in_specs=in_specs, out_specs=out_specs, check_vma=False)
```

time: 302 us -> 60.1 us (0.20); the launches traced: 298 us -> 59.9 us
  waiting for transfers between devices: 208 us -> 0 us
  Pallas kernels: 0 us -> 56.9 us
  local copies, waits for them, and re-layouts: 30.6 us -> 2.29 us
  between operations: 22.9 us -> 0.66 us
  other arithmetic: 15.4 us -> 0 us
  starting transfers between devices: 14.4 us -> 0 us
  matrix products: 5.87 us -> 0 us
    psum x1 -> x0, waiting for transfers between devices: 193 us -> none  [per_device(): summed = lax.psum(partial_value, 'pos')]
    pallas_call x0 -> x2, Pallas kernels: none -> 56.9 us  [the longest x1 49.7 us: per_device(): pl.pallas_call(combine_kernel, out_shape=planes, in_specs=[vmem] * 3, out...]
    ppermute x4 -> x0, waiting for transfers between devices: 15 us -> none  [the longest x1 9.59 us: padded(): before = lax.ppermute(last, axis, up)]
    ppermute x4 -> x0, starting transfers between devices: 14.4 us -> none  [the longest x2 10.7 us: shifted(): lax.ppermute(value, axis, [(source, source + steps) for source in range(i...]
    dynamic_update_slice x2 -> x0, local copies, waits for them, and re-layouts: 6.76 us -> none  [local_gradient(): lax.dynamic_update_slice(accumulated, region + gradient, starts)]
    unnamed x40 -> x1, local copies, waits for them, and re-layouts: 8.78 us -> 2.29 us
    dot_general x24 -> x0, matrix products: 5.87 us -> none  [right_pass(): result = jnp.dot(stacked, joined, preferred_element_type=jnp.float32)]
    scatter-add x2 -> x0, local copies, waits for them, and re-layouts: 4.66 us -> none  [the longest x1 2.4 us: add_strips(): result = result.at[..., extent - CORRELATION:].add(right_part)]
  transfers between devices with their start and end apart: 5 -> 0, of which waited for: 3 -> 0; matrix products, arithmetic and copies ran while one was open for 2% -> 0% of each run, Pallas kernels for 0% -> 0%
where the time goes in v1:
time: 60.1 us; the launch traced here: 59.9 us
  Pallas kernels  56.9 us (95%)
  local copies, waits for them, and re-layouts  2.29 us (4%)
  between operations  0.66 us (1%)
    pallas_call x1, Pallas kernels, per_device(): pl.pallas_call(combine_kernel, out_shape=planes, in_specs=[vmem] * 3, out...  49.7 us
    pallas_call x1, Pallas kernels, per_device(): pl.pallas_call(gradient_kernel, out_shape=planes, in_specs=[smem, smem] +...  7.22 us
    unnamed x1, local copies, waits for them, and re-layouts  2.29 us

profile of v1, /device:TPU:1, one launch (start us, length us, event | category | flops | bytes accessed | tf_op | source)
XLA Modules:
  0.0 59.9 jit_solution(11784444439628926272)
XLA Ops:
  0.7 7.2 %gradient.1.part_ref = f32[4,256,256]{2,1,0:T(8,128)} custom-call(s32[2,2]{1,0:T(2,128)} %bitcast.11, s32[1,1]{1,0:T(1,128)S(6)} %copy.10.count_ref, f32[2,256,256]{2,1,0:T(8,128)} %bitcast.6, f32[2,256,256]{2,1,0:T(8,128)} %bitcast.8, f32[2,3,128,128]{3,2,1,0:T(8,128)} %probe_ref.1, f32[2,128,128]{2,1,0:T(8,128)} %bitcast.10, ...), custom_call_target="tpu_custom_call" | custom-call | tf_op jit(solution)/shard_map/gradient/pallas_call | solution.py:287
  7.9 49.7 %combine.1 = f32[4,256,256]{2,1,0:T(8,128)} custom-call(f32[4,256,256]{2,1,0:T(8,128)} %gradient.1.part_ref, f32[2,256,256]{2,1,0:T(8,128)} %bitcast.7, f32[2,256,256]{2,1,0:T(8,128)} %bitcast.9), custom_call_target="tpu_custom_call" | custom-call | tf_op jit(solution)/shard_map/combine/pallas_call | solution.py:294
  57.6 2.3 %copy.11 = f32[1,2,2,256,256]{4,3,2,1,0:T(8,128)} copy(f32[1,2,2,256,256]{4,3,2,1,0:T(8,128)} %bitcast.5) | data formatting | bytes 2097152

commit v2 on v1

v2 whole, which is shorter than its diff:
```python
import functools
import math

import jax
import jax.numpy as jnp
import numpy as np
from jax import lax
from jax.experimental import pallas as pl
from jax.experimental.pallas import tpu as pltpu
from jax.sharding import PartitionSpec as P

MESH = pl.DeviceIdType.MESH
TILE = 256
WIN = 128
EDGE = 64
MODES = 3
LAYERS = 2
SLOTS = 2
STEP = 0.1
FRESNEL = 0.0123
SIN = (0.9999999957326958, -0.16666657991741893, 0.008333051059307331, -0.0001980907498047039, 2.605224199925007e-06)
COS = (0.9999999997806426, -0.49999999358456015, 0.04166663625748454, -0.001388836139270363, 2.476016095941152e-05, -2.6051488147238807e-07)


def make_tables():
    counter = np.arange(WIN)
    angles = (np.outer(counter, counter) % WIN).astype(np.float32) * np.float32(2.0 * math.pi / WIN)
    scaling = np.float32(1.0 / math.sqrt(WIN))
    f_re = (np.cos(angles) * scaling).astype(jnp.bfloat16)
    f_im = (-np.sin(angles) * scaling).astype(jnp.bfloat16)
    forward = np.block([[f_re, f_im], [-f_im, f_re]])
    inverse = np.block([[f_re, -f_im], [f_im, f_re]])
    centered = ((counter + WIN // 2) % WIN - WIN // 2).astype(np.float32)
    square = centered * centered
    phases = np.float32(-FRESNEL) * (square[:, None] + square[None, :])
    kernel = np.stack([np.cos(phases), np.sin(phases)]).astype(np.float32)
    return np.stack([forward, inverse]).astype(jnp.bfloat16), kernel


def horner(terms, u):
    total = jnp.full_like(u, terms[-1])
    for term in terms[-2::-1]:
        total = total * u + term
    return total


def polar(amplitude, phase):
    half = phase * 0.5
    u = half * half
    sine = half * horner(SIN, u)
    cosine = horner(COS, u)
    return amplitude - (2.0 * amplitude) * (sine * sine), (2.0 * amplitude) * (sine * cosine)


def times(a, b):
    return a[0] * b[0] - a[1] * b[1], a[0] * b[1] + a[1] * b[0]


def times_conj(a, b):
    return a[0] * b[0] + a[1] * b[1], a[1] * b[0] - a[0] * b[1]


def right_pass(waves, table):
    rows = [jnp.concatenate([re.astype(jnp.bfloat16), im.astype(jnp.bfloat16)], axis=1) for re, im in waves]
    result = jnp.dot(jnp.concatenate(rows, axis=0), table, preferred_element_type=jnp.float32)
    return [(result[i * WIN : (i + 1) * WIN, :WIN], result[i * WIN : (i + 1) * WIN, WIN:]) for i in range(len(waves))]


def left_pass(waves, table):
    columns = [jnp.concatenate([re.astype(jnp.bfloat16), im.astype(jnp.bfloat16)], axis=0) for re, im in waves]
    result = jnp.dot(table, jnp.concatenate(columns, axis=1), preferred_element_type=jnp.float32)
    return [(result[:WIN, i * WIN : (i + 1) * WIN], result[WIN:, i * WIN : (i + 1) * WIN]) for i in range(len(waves))]


def transform(waves, right, left):
    return left_pass(right_pass(waves, right), left)


def transform_back(waves, right, left):
    return right_pass(left_pass(waves, left), right)


def crop(ref, layer, row, column):
    rows = pltpu.roll(ref[layer], lax.rem(TILE - column, TILE), 1)[:, :WIN]
    return pltpu.roll(rows, lax.rem(TILE - row, TILE), 0)[:WIN]


def add_all(values):
    total = values[0]
    for value in values[1:]:
        total = total + value
    return total


def spread_out(value, row, column):
    wide = pltpu.roll(jnp.concatenate([value, jnp.zeros_like(value)], axis=1), column, 1)
    return pltpu.roll(jnp.concatenate([wide, jnp.zeros_like(wide)], axis=0), row, 0)


def sum_modes(pairs):
    return add_all([v[0] for v in pairs]), add_all([v[1] for v in pairs])


def fused_kernel(
    off_ref, count_ref, amp_ref, phase_ref, probe_ref, measured_ref, tables_ref, kernel_ref, out_ref,
    grad, pair, half, xin, block, zin, total, strips, strips_in, rows_in, send, recv,
):
    tile, pos = lax.axis_index("tile"), lax.axis_index("pos")
    tiles = lax.axis_size("tile")
    core, z_hi, x = lax.rem(pos, 2), lax.rem(pos // 2, 2), pos // 4
    z_lo = lax.rem(tile, 4)
    xs = [lax.rem(x + step, 4) for step in range(4)]

    def at(tile_step, x_, z_, core_):
        return {"tile": lax.rem(tile + tiles + tile_step, tiles), "pos": x_ * 4 + z_ * 2 + core_}

    sibling = at(0, x, z_hi, 1 - core)
    along_x = {step: at(0, xs[step], z_hi, core) for step in (1, 2, 3)}
    across = at(0, x, 1 - z_hi, core)
    after = at(1, x, jnp.where(z_lo == 3, 1 - z_hi, z_hi), core)
    before = at(-1, x, jnp.where(z_lo == 0, 1 - z_hi, z_hi), core)
    below = at(4, x, z_hi, core)
    above = at(-4, x, z_hi, core)

    partners = (sibling, along_x[1], along_x[3], along_x[2], across, after, before, below, above)
    barrier = pltpu.get_barrier_semaphore()
    for partner in partners:
        pl.semaphore_signal(barrier, inc=1, device_id=partner, device_id_type=MESH)

    started = []

    def push(chunk, index, src, dst, device):
        copy = pltpu.make_async_remote_copy(
            src_ref=src, dst_ref=dst, send_sem=send.at[chunk, index], recv_sem=recv.at[chunk, index],
            device_id=device, device_id_type=MESH,
        )
        copy.start()
        started.append(copy)
        return copy

    def rows_of(x_, core_):
        return pl.ds(pl.multiple_of(lax.rem(x_, 2) * 32 + core_ * 16, 16), 16)

    def flat(value):
        return value.reshape(EDGE, TILE)

    forward, inverse = tables_ref[0], tables_ref[1]
    slots = range(SLOTS)
    rows = [off_ref[slot, 0] for slot in slots]
    columns = [off_ref[slot, 1] for slot in slots]
    lives = [(count_ref[0, 0] - slot).astype(jnp.float32) for slot in slots]
    lives = [jnp.clip(jnp.full((1, TILE), live), 0.0, 1.0) for live in lives]

    def kernel():
        return kernel_ref[0], kernel_ref[1]

    def probe(m):
        return probe_ref[0, m], probe_ref[1, m]

    def collect(layer, grads):
        for part in range(2):
            parts = [spread_out(grads[slot][part], rows[slot], columns[slot]) * lives[slot] for slot in slots]
            grad[layer, part] = (parts[0] + parts[1]).reshape(4, EDGE, TILE)

    def each(stage, *lists):
        return [stage(*items) for items in zip(*lists)]

    modes = range(MODES)
    layers = []
    for slot in slots:
        layers.append(
            [
                polar(
                    crop(amp_ref, layer, rows[slot], columns[slot]),
                    crop(phase_ref, layer, rows[slot], columns[slot]),
                )
                for layer in range(LAYERS)
            ]
        )
    waves = [[times(probe(m), layers[slot][0]) for m in modes] for slot in slots]
    waves = each(lambda w: right_pass(w, forward), waves)
    waves = each(lambda w: left_pass(w, inverse), waves)
    waves = each(lambda w: [times(v, kernel()) for v in w], waves)
    waves = each(lambda w: right_pass(w, inverse), waves)
    returned = each(lambda w: left_pass(w, forward), waves)
    waves = each(lambda w, o: [times(v, o[1]) for v in w], returned, layers)
    waves = each(lambda w: right_pass(w, forward), waves)
    far = each(lambda w: left_pass(w, inverse), waves)

    def pull(slot, w):
        misfit = add_all([re * re + im * im for re, im in w]) - measured_ref[slot]
        twice = misfit + misfit
        return [(twice * re, twice * im) for re, im in w]

    waves = each(pull, slots, far)
    waves = each(lambda w: left_pass(w, forward), waves)
    waves = each(lambda w: right_pass(w, inverse), waves)
    collect(1, [sum_modes([times_conj(g, r) for g, r in zip(waves[slot], returned[slot])]) for slot in slots])

    def swap_pair(chunk):
        copies = []
        for step in (2, 1, 3, 0):
            owner = xs[step]
            src = grad.at[chunk, owner // 2, :, rows_of(owner, 1 - core)]
            copies.append((step, push(chunk, step, src, pair.at[chunk, step], sibling)))
        return copies

    def spread_x(chunk, swaps):
        copies = []
        for step, swap in swaps:
            swap.wait_recv()
            owner = xs[step]
            half[chunk, step] = grad[chunk, owner // 2, :, rows_of(owner, core), :] + pair[chunk, step]
            if step:
                copies.append(push(chunk, 3 + step, half.at[chunk, step], xin.at[chunk, step - 1], along_x[step]))
        return copies

    def swap_z(chunk, copies):
        for copy in copies:
            copy.wait_recv()
        block[chunk] = half[chunk, 0] + (xin[chunk, 0] + xin[chunk, 2] + xin[chunk, 1])
        return push(chunk, 7, block.at[chunk], zin.at[chunk], across)

    low = lax.broadcasted_iota(jnp.int32, (32, WIN), 1) < EDGE

    def swap_strips(chunk, copy):
        copy.wait_recv()
        total[chunk] = block[chunk] + zin[chunk]
        copies = [
            push(chunk, 8, total.at[chunk, 3], rows_in.at[chunk, 0], below),
            push(chunk, 9, total.at[chunk, 0], rows_in.at[chunk, 1], above),
        ]
        value = flat(total[chunk])
        left, right = value[:, :WIN], value[:, WIN:]
        strips[chunk, 0] = jnp.where(low, pltpu.roll(right[:32], EDGE, 1), right[32:])
        strips[chunk, 1] = jnp.where(low, left[:32], pltpu.roll(left[32:], EDGE, 1))
        copies.append(push(chunk, 10, strips.at[chunk, 0], strips_in.at[chunk, 0], after))
        copies.append(push(chunk, 11, strips.at[chunk, 1], strips_in.at[chunk, 1], before))
        return copies

    own_rows = rows_of(x, core)
    offset = lax.rem(x, 2) * 32 + core * 16

    def share(chunk, index, step, device):
        owner = xs[step]
        view = out_ref.at[owner // 2, chunk, :, rows_of(owner, core)]
        return push(chunk, index, view, view, device)

    def object_block(layer):
        def read(ref):
            return jnp.concatenate(
                [ref[layer, pl.ds(pl.multiple_of(p * EDGE + offset, 16), 16), :] for p in range(4)], axis=0
            )

        both = polar(read(amp_ref), read(phase_ref))
        return jnp.where(x < 2, both[0], both[1])

    def update(chunk, copies, base):
        for copy in copies:
            copy.wait_recv()
        from_left = jnp.where(tile > 0, strips_in[chunk, 0], 0.0)
        from_right = jnp.where(tile < tiles - 1, strips_in[chunk, 1], 0.0)
        left = jnp.concatenate(
            [jnp.where(low, from_left, 0.0), jnp.where(low, pltpu.roll(from_left, EDGE, 1), 0.0)], axis=0
        )
        right = jnp.concatenate(
            [jnp.where(low, 0.0, pltpu.roll(from_right, EDGE, 1)), jnp.where(low, 0.0, from_right)], axis=0
        )
        top = jnp.where(tile >= 4, rows_in[chunk, 0], 0.0)
        bottom = jnp.where(tile < tiles - 4, rows_in[chunk, 1], 0.0)
        ends = jnp.concatenate([top, jnp.zeros((32, TILE), jnp.float32), bottom], axis=0)
        combined = flat(total[chunk]) + jnp.concatenate([left, right], axis=1) + ends
        out_ref[x // 2, chunk, :, own_rows, :] = (base - STEP * combined).reshape(4, 16, TILE)
        remote = [(step, share(chunk, 11 + step, 0, along_x[step])) for step in (2, 1, 3)]
        return remote, [share(chunk, 15, 0, sibling)]

    def relay(chunk, remote, local):
        for step, copy in remote:
            copy.wait_recv()
            local.append(share(chunk, 15 + step, 4 - step, sibling))

    pl.semaphore_wait(barrier, len(partners))
    pairs_late = swap_pair(1)
    waves = each(lambda w, o: [times_conj(v, o[1]) for v in w], waves, layers)
    waves = each(lambda w: left_pass(w, inverse), waves)
    waves = each(lambda w: right_pass(w, forward), waves)
    waves = each(lambda w: [times_conj(v, kernel()) for v in w], waves)
    xs_late = spread_x(1, pairs_late)
    waves = each(lambda w: left_pass(w, forward), waves)
    waves = each(lambda w: right_pass(w, inverse), waves)
    collect(0, [sum_modes([times_conj(waves[slot][m], probe(m)) for m in modes]) for slot in slots])
    pairs_early = swap_pair(0)
    z_late = swap_z(1, xs_late)
    xs_early = spread_x(0, pairs_early)
    base_late = object_block(1)
    z_early = swap_z(0, xs_early)
    base_early = object_block(0)
    strips_late = swap_strips(1, z_late)
    strips_early = swap_strips(0, z_early)
    remote_late, local_late = update(1, strips_late, base_late)
    remote_early, local_early = update(0, strips_early, base_early)
    relay(1, remote_late, local_late)
    relay(0, remote_early, local_early)
    for copy in local_late + local_early:
        copy.wait_recv()
    for copy in started:
        copy.wait_send()


def per_device(amplitude, phase_map, probe_modes, offsets, pos_counts, measured):
    tables, kernel = make_tables()
    vmem = pl.BlockSpec(memory_space=pltpu.VMEM)
    smem = pl.BlockSpec(memory_space=pltpu.SMEM)
    f32 = jnp.float32
    updated = pl.pallas_call(
        fused_kernel,
        out_shape=jax.ShapeDtypeStruct((2, LAYERS, 4, EDGE, TILE), f32),
        in_specs=[smem, smem] + [vmem] * 6,
        out_specs=vmem,
        scratch_shapes=[
            pltpu.VMEM((LAYERS, 2, 4, EDGE, TILE), f32),
            pltpu.VMEM((LAYERS, 4, 4, 16, TILE), f32),
            pltpu.VMEM((LAYERS, 4, 4, 16, TILE), f32),
            pltpu.VMEM((LAYERS, 3, 4, 16, TILE), f32),
            pltpu.VMEM((LAYERS, 4, 16, TILE), f32),
            pltpu.VMEM((LAYERS, 4, 16, TILE), f32),
            pltpu.VMEM((LAYERS, 4, 16, TILE), f32),
            pltpu.VMEM((LAYERS, 2, 32, WIN), f32),
            pltpu.VMEM((LAYERS, 2, 32, WIN), f32),
            pltpu.VMEM((LAYERS, 2, 16, TILE), f32),
            pltpu.SemaphoreType.DMA((LAYERS, 19)),
            pltpu.SemaphoreType.DMA((LAYERS, 19)),
        ],
        compiler_params=pltpu.CompilerParams(collective_id=0, has_side_effects=True),
        name="gradient_and_combine",
    )(offsets[0], pos_counts, amplitude[0], phase_map[0], probe_modes, measured[0], jnp.asarray(tables), jnp.asarray(kernel))
    return updated.reshape(1, 2, LAYERS, TILE, TILE)


def solution(mesh):
    in_specs = (
        P("tile", None, None, None),
        P("tile", None, None, None),
        P(),
        P("tile", "pos", None),
        P("tile", "pos"),
        P("tile", "pos", None, None),
    )
    out_specs = P("tile", None, None, None, None)
    return jax.shard_map(per_device, mesh=mesh, in_specs=in_specs, out_specs=out_specs, check_vma=False)
```

time: 60.1 us -> 49.6 us (0.83)
  Pallas kernels: 56.9 us -> 46.5 us
    pallas_call x2 -> x1, Pallas kernels: 56.9 us -> 46.5 us  [per_device(): pl.pallas_call(fused_kernel, out_shape=jax.ShapeDtypeStruct((2, LAYERS, 4...]
where the time goes in v2:
time: 49.6 us; the launch traced here: 49.4 us
  Pallas kernels  46.5 us (94%)
  local copies, waits for them, and re-layouts  2.29 us (5%)
  between operations  0.66 us (1%)
    pallas_call x1, Pallas kernels, per_device(): pl.pallas_call(fused_kernel, out_shape=jax.ShapeDtypeStruct((2, LAYERS, 4...  46.5 us
    unnamed x1, local copies, waits for them, and re-layouts  2.29 us

profile of v2, /device:TPU:1, one launch (start us, length us, event | category | flops | bytes accessed | tf_op | source)
XLA Modules:
  0.0 49.4 jit_solution(7968004527908129153)
XLA Ops:
  0.7 46.5 %gradient_and_combine.1 = f32[2,2,4,64,256]{4,3,2,1,0:T(8,128)} custom-call(s32[2,2]{1,0:T(2,128)} %bitcast.9, s32[1,1]{1,0:T(1,128)S(6)} %copy.10.count_ref, f32[2,256,256]{2,1,0:T(8,128)} %bitcast.6, f32[2,256,256]{2,1,0:T(8,128)} %bitcast.7, f32[2,3,128,128]{3,2,1,0:T(8,128)} %probe_ref.1, f32[2,128,128]{2,1,0:T(8,128)} %bitcast.8, ...), custom_call_target="tpu_custom_call" | custom-call | tf_op jit(solution)/shard_map/gradient_and_combine/pallas_call | solution.py:315
  47.2 2.3 %copy.11 = f32[1,2,2,256,256]{4,3,2,1,0:T(8,128)} copy(f32[1,2,2,256,256]{4,3,2,1,0:T(8,128)} %bitcast.5) | data formatting | bytes 2097152

commit v3 on v2

--- a/solution.py
+++ b/solution.py
@@ -16,6 +16,8 @@
 MODES = 3
 LAYERS = 2
 SLOTS = 2
+SPAN = WIN + 8
+LEAD = (TILE - SPAN) // 8
 STEP = 0.1
 FRESNEL = 0.0123
 SIN = (0.9999999957326958, -0.16666657991741893, 0.008333051059307331, -0.0001980907498047039, 2.605224199925007e-06)
@@ -80,9 +82,10 @@
     return right_pass(left_pass(waves, left), right)
 
 
-def crop(ref, layer, row, column):
-    rows = pltpu.roll(ref[layer], lax.rem(TILE - column, TILE), 1)[:, :WIN]
-    return pltpu.roll(rows, lax.rem(TILE - row, TILE), 0)[:WIN]
+def crop(ref, layer, group, shift, column):
+    rows = jnp.concatenate([ref[layer, group + j] for j in range(SPAN // 8)], axis=0)
+    rows = pltpu.roll(rows, lax.rem(TILE - column, TILE), 1)[:, :WIN]
+    return pltpu.roll(rows, lax.rem(SPAN - shift, SPAN), 0)[:WIN]
 
 
 def add_all(values):
@@ -92,9 +95,10 @@
     return total
 
 
-def spread_out(value, row, column):
-    wide = pltpu.roll(jnp.concatenate([value, jnp.zeros_like(value)], axis=1), column, 1)
-    return pltpu.roll(jnp.concatenate([wide, jnp.zeros_like(wide)], axis=0), row, 0)
+def spread_out(value, shift, column):
+    tall = jnp.concatenate([value, jnp.zeros((SPAN - WIN, WIN), value.dtype)], axis=0)
+    tall = pltpu.roll(tall, shift, 0)
+    return pltpu.roll(jnp.concatenate([tall, jnp.zeros_like(tall)], axis=1), column, 1)
 
 
 def sum_modes(pairs):
@@ -103,7 +107,7 @@
 
 def fused_kernel(
     off_ref, count_ref, amp_ref, phase_ref, probe_ref, measured_ref, tables_ref, kernel_ref, out_ref,
-    grad, pair, half, xin, block, zin, total, strips, strips_in, rows_in, send, recv,
+    pad, grad, pair, half, xin, block, zin, total, strips, strips_in, rows_in, send, recv,
 ):
     tile, pos = lax.axis_index("tile"), lax.axis_index("pos")
     tiles = lax.axis_size("tile")
@@ -146,10 +150,15 @@
 
     forward, inverse = tables_ref[0], tables_ref[1]
     slots = range(SLOTS)
-    rows = [off_ref[slot, 0] for slot in slots]
-    columns = [off_ref[slot, 1] for slot in slots]
+    groups, shifts, columns = [], [], []
     lives = [(count_ref[0, 0] - slot).astype(jnp.float32) for slot in slots]
-    lives = [jnp.clip(jnp.full((1, TILE), live), 0.0, 1.0) for live in lives]
+    lives = [jnp.clip(jnp.full((1, WIN), live), 0.0, 1.0) for live in lives]
+    for slot in slots:
+        row = off_ref[slot, 0]
+        group = lax.shift_right_logical(row - lax.shift_right_logical(row, 7), 3)
+        groups.append(group)
+        shifts.append(row - group * 8)
+        columns.append(off_ref[slot, 1])
 
     def kernel():
         return kernel_ref[0], kernel_ref[1]
@@ -157,10 +166,24 @@
     def probe(m):
         return probe_ref[0, m], probe_ref[1, m]
 
-    def collect(layer, grads):
+    def deposit(slot, layer, grads):
         for part in range(2):
-            parts = [spread_out(grads[slot][part], rows[slot], columns[slot]) * lives[slot] for slot in slots]
-            grad[layer, part] = (parts[0] + parts[1]).reshape(4, EDGE, TILE)
+            value = grads[part] * lives[slot]
+            placed = spread_out(value, shifts[slot], columns[slot])
+            pad[slot, part, layer, LEAD : LEAD + SPAN // 8] = placed.reshape(SPAN // 8, 8, TILE)
+
+    def collect(layer):
+        for part in range(2):
+            for r in range(TILE // 8):
+                first, second = [pad[slot, part, layer, LEAD - groups[slot] + r] for slot in slots]
+                grad[layer, part, r // 8, r % 8 * 8 : r % 8 * 8 + 8, :] = first + second
+
+    empty = jnp.zeros((LEAD, 8, TILE), jnp.float32)
+    for slot in slots:
+        for part in range(2):
+            for layer in range(LAYERS):
+                pad[slot, part, layer, 0:LEAD] = empty
+                pad[slot, part, layer, LEAD + SPAN // 8 :] = empty
 
     def each(stage, *lists):
         return [stage(*items) for items in zip(*lists)]
@@ -171,8 +194,8 @@
         layers.append(
             [
                 polar(
-                    crop(amp_ref, layer, rows[slot], columns[slot]),
-                    crop(phase_ref, layer, rows[slot], columns[slot]),
+                    crop(amp_ref, layer, groups[slot], shifts[slot], columns[slot]),
+                    crop(phase_ref, layer, groups[slot], shifts[slot], columns[slot]),
                 )
                 for layer in range(LAYERS)
             ]
@@ -195,7 +218,9 @@
     waves = each(pull, slots, far)
     waves = each(lambda w: left_pass(w, forward), waves)
     waves = each(lambda w: right_pass(w, inverse), waves)
-    collect(1, [sum_modes([times_conj(g, r) for g, r in zip(waves[slot], returned[slot])]) for slot in slots])
+    for slot in slots:
+        deposit(slot, 1, sum_modes([times_conj(g, r) for g, r in zip(waves[slot], returned[slot])]))
+    collect(1)
 
     def swap_pair(chunk):
         copies = []
@@ -239,7 +264,7 @@
         return copies
 
     own_rows = rows_of(x, core)
-    offset = lax.rem(x, 2) * 32 + core * 16
+    offset = lax.rem(x, 2) * 4 + core * 2
 
     def share(chunk, index, step, device):
         owner = xs[step]
@@ -249,7 +274,7 @@
     def object_block(layer):
         def read(ref):
             return jnp.concatenate(
-                [ref[layer, pl.ds(pl.multiple_of(p * EDGE + offset, 16), 16), :] for p in range(4)], axis=0
+                [ref[layer, pl.ds(p * 8 + offset, 2)].reshape(16, TILE) for p in range(4)], axis=0
             )
 
         both = polar(read(amp_ref), read(phase_ref))
@@ -288,7 +313,9 @@
     xs_late = spread_x(1, pairs_late)
     waves = each(lambda w: left_pass(w, forward), waves)
     waves = each(lambda w: right_pass(w, inverse), waves)
-    collect(0, [sum_modes([times_conj(waves[slot][m], probe(m)) for m in modes]) for slot in slots])
+    for slot in slots:
+        deposit(slot, 0, sum_modes([times_conj(waves[slot][m], probe(m)) for m in modes]))
+    collect(0)
     pairs_early = swap_pair(0)
     z_late = swap_z(1, xs_late)
     xs_early = spread_x(0, pairs_early)
@@ -307,6 +334,10 @@
         copy.wait_send()
 
 
+def grouped(tile_array):
+    return tile_array.reshape(LAYERS, TILE // 8, 8, TILE)
+
+
 def per_device(amplitude, phase_map, probe_modes, offsets, pos_counts, measured):
     tables, kernel = make_tables()
     vmem = pl.BlockSpec(memory_space=pltpu.VMEM)
@@ -318,6 +349,7 @@
         in_specs=[smem, smem] + [vmem] * 6,
         out_specs=vmem,
         scratch_shapes=[
+            pltpu.VMEM((SLOTS, 2, LAYERS, 2 * LEAD + SPAN // 8, 8, TILE), f32),
             pltpu.VMEM((LAYERS, 2, 4, EDGE, TILE), f32),
             pltpu.VMEM((LAYERS, 4, 4, 16, TILE), f32),
             pltpu.VMEM((LAYERS, 4, 4, 16, TILE), f32),
@@ -333,7 +365,7 @@
         ],
         compiler_params=pltpu.CompilerParams(collective_id=0, has_side_effects=True),
         name="gradient_and_combine",
-    )(offsets[0], pos_counts, amplitude[0], phase_map[0], probe_modes, measured[0], jnp.asarray(tables), jnp.asarray(kernel))
+    )(offsets[0], pos_counts, grouped(amplitude), grouped(phase_map), probe_modes, measured[0], jnp.asarray(tables), jnp.asarray(kernel))
     return updated.reshape(1, 2, LAYERS, TILE, TILE)
 
 

time: 49.6 us -> 49.6 us (level)
  no operation moved by 1% of the time
where the time goes in v3:
time: 49.6 us; the launch traced here: 49.5 us
  Pallas kernels  46.5 us (94%)
  local copies, waits for them, and re-layouts  2.29 us (5%)
  between operations  0.66 us (1%)
    pallas_call x1, Pallas kernels, per_device(): pl.pallas_call(fused_kernel, out_shape=jax.ShapeDtypeStruct((2, LAYERS, 4...  46.5 us
    unnamed x1, local copies, waits for them, and re-layouts  2.29 us

profile of v3, /device:TPU:1, one launch (start us, length us, event | category | flops | bytes accessed | tf_op | source)
XLA Modules:
  0.0 49.5 jit_solution(17144784039243981789)
XLA Ops:
  0.7 46.5 %gradient_and_combine.1 = f32[2,2,4,64,256]{4,3,2,1,0:T(8,128)} custom-call(s32[2,2]{1,0:T(2,128)} %bitcast.9, s32[1,1]{1,0:T(1,128)S(6)} %copy.10.count_ref, f32[2,32,8,256]{3,2,1,0:T(8,128)} %bitcast.6, f32[2,32,8,256]{3,2,1,0:T(8,128)} %bitcast.7, f32[2,3,128,128]{3,2,1,0:T(8,128)} %probe_ref.1, f32[2,128,128]{2,1,0:T(8,128)} %bitcast.8, ...), custom_call_target="tpu_custom_call" | custom-call | tf_op jit(solution)/shard_map/gradient_and_combine/pallas_call | solution.py:346
  47.2 2.3 %copy.11 = f32[1,2,2,256,256]{4,3,2,1,0:T(8,128)} copy(f32[1,2,2,256,256]{4,3,2,1,0:T(8,128)} %bitcast.5) | data formatting | bytes 2097152

commit v4 on v3

--- a/solution.py
+++ b/solution.py
@@ -18,6 +18,9 @@
 SLOTS = 2
 SPAN = WIN + 8
 LEAD = (TILE - SPAN) // 8
+SUBS = 2
+HIGH = 16 // SUBS
+CHUNKS = LAYERS * SUBS
 STEP = 0.1
 FRESNEL = 0.0123
 SIN = (0.9999999957326958, -0.16666657991741893, 0.008333051059307331, -0.0001980907498047039, 2.605224199925007e-06)
@@ -142,11 +145,11 @@
         started.append(copy)
         return copy
 
-    def rows_of(x_, core_):
-        return pl.ds(pl.multiple_of(lax.rem(x_, 2) * 32 + core_ * 16, 16), 16)
+    def rows_of(x_, core_, sub):
+        return pl.ds(pl.multiple_of(lax.rem(x_, 2) * 32 + core_ * 16 + sub * HIGH, HIGH), HIGH)
 
     def flat(value):
-        return value.reshape(EDGE, TILE)
+        return value.reshape(4 * HIGH, TILE)
 
     forward, inverse = tables_ref[0], tables_ref[1]
     slots = range(SLOTS)
@@ -223,19 +226,21 @@
     collect(1)
 
     def swap_pair(chunk):
+        layer, sub = divmod(chunk, SUBS)
         copies = []
         for step in (2, 1, 3, 0):
             owner = xs[step]
-            src = grad.at[chunk, owner // 2, :, rows_of(owner, 1 - core)]
+            src = grad.at[layer, owner // 2, :, rows_of(owner, 1 - core, sub)]
             copies.append((step, push(chunk, step, src, pair.at[chunk, step], sibling)))
         return copies
 
     def spread_x(chunk, swaps):
+        layer, sub = divmod(chunk, SUBS)
         copies = []
         for step, swap in swaps:
             swap.wait_recv()
             owner = xs[step]
-            half[chunk, step] = grad[chunk, owner // 2, :, rows_of(owner, core), :] + pair[chunk, step]
+            half[chunk, step] = grad[layer, owner // 2, :, rows_of(owner, core, sub), :] + pair[chunk, step]
             if step:
                 copies.append(push(chunk, 3 + step, half.at[chunk, step], xin.at[chunk, step - 1], along_x[step]))
         return copies
@@ -246,7 +251,7 @@
         block[chunk] = half[chunk, 0] + (xin[chunk, 0] + xin[chunk, 2] + xin[chunk, 1])
         return push(chunk, 7, block.at[chunk], zin.at[chunk], across)
 
-    low = lax.broadcasted_iota(jnp.int32, (32, WIN), 1) < EDGE
+    low = lax.broadcasted_iota(jnp.int32, (2 * HIGH, WIN), 1) < EDGE
 
     def swap_strips(chunk, copy):
         copy.wait_recv()
@@ -257,30 +262,32 @@
         ]
         value = flat(total[chunk])
         left, right = value[:, :WIN], value[:, WIN:]
-        strips[chunk, 0] = jnp.where(low, pltpu.roll(right[:32], EDGE, 1), right[32:])
-        strips[chunk, 1] = jnp.where(low, left[:32], pltpu.roll(left[32:], EDGE, 1))
+        strips[chunk, 0] = jnp.where(low, pltpu.roll(right[: 2 * HIGH], EDGE, 1), right[2 * HIGH :])
+        strips[chunk, 1] = jnp.where(low, left[: 2 * HIGH], pltpu.roll(left[2 * HIGH :], EDGE, 1))
         copies.append(push(chunk, 10, strips.at[chunk, 0], strips_in.at[chunk, 0], after))
         copies.append(push(chunk, 11, strips.at[chunk, 1], strips_in.at[chunk, 1], before))
         return copies
 
-    own_rows = rows_of(x, core)
-    offset = lax.rem(x, 2) * 4 + core * 2
-
     def share(chunk, index, step, device):
+        layer, sub = divmod(chunk, SUBS)
         owner = xs[step]
-        view = out_ref.at[owner // 2, chunk, :, rows_of(owner, core)]
+        view = out_ref.at[owner // 2, layer, :, rows_of(owner, core, sub)]
         return push(chunk, index, view, view, device)
 
-    def object_block(layer):
+    def object_block(chunk):
+        layer, sub = divmod(chunk, SUBS)
+        first = lax.rem(x, 2) * 4 + core * 2 + sub * (HIGH // 8)
+
         def read(ref):
             return jnp.concatenate(
-                [ref[layer, pl.ds(p * 8 + offset, 2)].reshape(16, TILE) for p in range(4)], axis=0
+                [ref[layer, pl.ds(p * 8 + first, HIGH // 8)].reshape(HIGH, TILE) for p in range(4)], axis=0
             )
 
         both = polar(read(amp_ref), read(phase_ref))
         return jnp.where(x < 2, both[0], both[1])
 
     def update(chunk, copies, base):
+        layer, sub = divmod(chunk, SUBS)
         for copy in copies:
             copy.wait_recv()
         from_left = jnp.where(tile > 0, strips_in[chunk, 0], 0.0)
@@ -293,9 +300,9 @@
         )
         top = jnp.where(tile >= 4, rows_in[chunk, 0], 0.0)
         bottom = jnp.where(tile < tiles - 4, rows_in[chunk, 1], 0.0)
-        ends = jnp.concatenate([top, jnp.zeros((32, TILE), jnp.float32), bottom], axis=0)
+        ends = jnp.concatenate([top, jnp.zeros((2 * HIGH, TILE), jnp.float32), bottom], axis=0)
         combined = flat(total[chunk]) + jnp.concatenate([left, right], axis=1) + ends
-        out_ref[x // 2, chunk, :, own_rows, :] = (base - STEP * combined).reshape(4, 16, TILE)
+        out_ref[x // 2, layer, :, rows_of(x, core, sub), :] = (base - STEP * combined).reshape(4, HIGH, TILE)
         remote = [(step, share(chunk, 11 + step, 0, along_x[step])) for step in (2, 1, 3)]
         return remote, [share(chunk, 15, 0, sibling)]
 
@@ -303,33 +310,34 @@
         for step, copy in remote:
             copy.wait_recv()
             local.append(share(chunk, 15 + step, 4 - step, sibling))
-
+        return local
+
+    late = list(range(SUBS, CHUNKS))
+    early = list(range(SUBS))
+    order = late + early
     pl.semaphore_wait(barrier, len(partners))
-    pairs_late = swap_pair(1)
+    swaps = {chunk: swap_pair(chunk) for chunk in late}
     waves = each(lambda w, o: [times_conj(v, o[1]) for v in w], waves, layers)
     waves = each(lambda w: left_pass(w, inverse), waves)
     waves = each(lambda w: right_pass(w, forward), waves)
     waves = each(lambda w: [times_conj(v, kernel()) for v in w], waves)
-    xs_late = spread_x(1, pairs_late)
     waves = each(lambda w: left_pass(w, forward), waves)
+    sums = {chunk: spread_x(chunk, swaps[chunk]) for chunk in late}
     waves = each(lambda w: right_pass(w, inverse), waves)
     for slot in slots:
         deposit(slot, 0, sum_modes([times_conj(waves[slot][m], probe(m)) for m in modes]))
     collect(0)
-    pairs_early = swap_pair(0)
-    z_late = swap_z(1, xs_late)
-    xs_early = spread_x(0, pairs_early)
-    base_late = object_block(1)
-    z_early = swap_z(0, xs_early)
-    base_early = object_block(0)
-    strips_late = swap_strips(1, z_late)
-    strips_early = swap_strips(0, z_early)
-    remote_late, local_late = update(1, strips_late, base_late)
-    remote_early, local_early = update(0, strips_early, base_early)
-    relay(1, remote_late, local_late)
-    relay(0, remote_early, local_early)
-    for copy in local_late + local_early:
-        copy.wait_recv()
+    swaps.update({chunk: swap_pair(chunk) for chunk in early})
+    bases = {chunk: object_block(chunk) for chunk in order}
+    for chunk in early:
+        sums[chunk] = spread_x(chunk, swaps[chunk])
+    blocks = {chunk: swap_z(chunk, sums[chunk]) for chunk in order}
+    edges = {chunk: swap_strips(chunk, blocks[chunk]) for chunk in order}
+    shares = {chunk: update(chunk, edges[chunk], bases[chunk]) for chunk in order}
+    ends = [relay(chunk, *shares[chunk]) for chunk in order]
+    for local in ends:
+        for copy in local:
+            copy.wait_recv()
     for copy in started:
         copy.wait_send()
 
@@ -345,23 +353,23 @@
     f32 = jnp.float32
     updated = pl.pallas_call(
         fused_kernel,
-        out_shape=jax.ShapeDtypeStruct((2, LAYERS, 4, EDGE, TILE), f32),
+        out_shape=pltpu.VMEM((2, LAYERS, 4, EDGE, TILE), f32),
         in_specs=[smem, smem] + [vmem] * 6,
         out_specs=vmem,
         scratch_shapes=[
             pltpu.VMEM((SLOTS, 2, LAYERS, 2 * LEAD + SPAN // 8, 8, TILE), f32),
             pltpu.VMEM((LAYERS, 2, 4, EDGE, TILE), f32),
-            pltpu.VMEM((LAYERS, 4, 4, 16, TILE), f32),
-            pltpu.VMEM((LAYERS, 4, 4, 16, TILE), f32),
-            pltpu.VMEM((LAYERS, 3, 4, 16, TILE), f32),
-            pltpu.VMEM((LAYERS, 4, 16, TILE), f32),
-            pltpu.VMEM((LAYERS, 4, 16, TILE), f32),
-            pltpu.VMEM((LAYERS, 4, 16, TILE), f32),
-            pltpu.VMEM((LAYERS, 2, 32, WIN), f32),
-            pltpu.VMEM((LAYERS, 2, 32, WIN), f32),
-            pltpu.VMEM((LAYERS, 2, 16, TILE), f32),
-            pltpu.SemaphoreType.DMA((LAYERS, 19)),
-            pltpu.SemaphoreType.DMA((LAYERS, 19)),
+            pltpu.VMEM((CHUNKS, 4, 4, HIGH, TILE), f32),
+            pltpu.VMEM((CHUNKS, 4, 4, HIGH, TILE), f32),
+            pltpu.VMEM((CHUNKS, 3, 4, HIGH, TILE), f32),
+            pltpu.VMEM((CHUNKS, 4, HIGH, TILE), f32),
+            pltpu.VMEM((CHUNKS, 4, HIGH, TILE), f32),
+            pltpu.VMEM((CHUNKS, 4, HIGH, TILE), f32),
+            pltpu.VMEM((CHUNKS, 2, 2 * HIGH, WIN), f32),
+            pltpu.VMEM((CHUNKS, 2, 2 * HIGH, WIN), f32),
+            pltpu.VMEM((CHUNKS, 2, HIGH, TILE), f32),
+            pltpu.SemaphoreType.DMA((CHUNKS, 19)),
+            pltpu.SemaphoreType.DMA((CHUNKS, 19)),
         ],
         compiler_params=pltpu.CompilerParams(collective_id=0, has_side_effects=True),
         name="gradient_and_combine",

time: 49.6 us -> 43.6 us (0.88)
  Pallas kernels: 46.5 us -> 41.8 us
  local copies, waits for them, and re-layouts: 2.29 us -> 0.97 us
    pallas_call x1, Pallas kernels: 46.5 us -> 41.8 us  [per_device(): pl.pallas_call(fused_kernel, out_shape=pltpu.VMEM((2, LAYERS, 4, EDGE, TI...]
    unnamed x1, local copies, waits for them, and re-layouts: 2.29 us -> 0.97 us
where the time goes in v4:
time: 43.6 us; the launch traced here: 43.5 us
  Pallas kernels  41.8 us (96%)
  local copies, waits for them, and re-layouts  0.97 us (2%)
  between operations  0.66 us (2%)
    pallas_call x1, Pallas kernels, per_device(): pl.pallas_call(fused_kernel, out_shape=pltpu.VMEM((2, LAYERS, 4, EDGE, TI...  41.8 us
    unnamed x1, local copies, waits for them, and re-layouts  0.97 us

profile of v4, /device:TPU:1, one launch (start us, length us, event | category | flops | bytes accessed | tf_op | source)
XLA Modules:
  0.0 43.5 jit_solution(10375354725207632300)
XLA Ops:
  0.7 41.8 %gradient_and_combine.1 = f32[2,2,4,64,256]{4,3,2,1,0:T(8,128)S(1)} custom-call(s32[2,2]{1,0:T(2,128)} %bitcast.9, s32[1,1]{1,0:T(1,128)S(6)} %copy.11.count_ref, f32[2,32,8,256]{3,2,1,0:T(8,128)} %bitcast.6, f32[2,32,8,256]{3,2,1,0:T(8,128)} %bitcast.7, f32[2,3,128,128]{3,2,1,0:T(8,128)} %probe_ref.1, f32[2,128,128]{2,1,0:T(8,128)} %bitcast.8, ...), custom_call_target="tpu_custom_call" | custom-call | tf_op jit(solution)/shard_map/gradient_and_combine/pallas_call | solution.py:354
  42.5 1.0 %copy.10 = f32[1,2,2,256,256]{4,3,2,1,0:T(8,128)} copy(f32[1,2,2,256,256]{4,3,2,1,0:T(8,128)S(1)} %bitcast.5) | data formatting | bytes 2097152

commit v5 on v4

--- a/solution.py
+++ b/solution.py
@@ -86,9 +86,16 @@
 
 
 def crop(ref, layer, group, shift, column):
-    rows = jnp.concatenate([ref[layer, group + j] for j in range(SPAN // 8)], axis=0)
-    rows = pltpu.roll(rows, lax.rem(TILE - column, TILE), 1)[:, :WIN]
-    return pltpu.roll(rows, lax.rem(SPAN - shift, SPAN), 0)[:WIN]
+    lane = lax.broadcasted_iota(jnp.int32, (8, WIN), 1)
+    sublane = lax.broadcasted_iota(jnp.int32, (8, WIN), 0)
+    rows = []
+    for j in range(SPAN // 8):
+        row = ref[layer, group + j]
+        rows.append(pltpu.roll(jnp.where(lane >= column, row[:, :WIN], row[:, WIN:]), (WIN - column) & (WIN - 1), 1))
+    picked = [
+        pltpu.roll(jnp.where(sublane >= shift, rows[j], rows[j + 1]), (8 - shift) & 7, 0) for j in range(WIN // 8)
+    ]
+    return jnp.concatenate(picked, axis=0)
 
 
 def add_all(values):
@@ -99,9 +106,17 @@
 
 
 def spread_out(value, shift, column):
-    tall = jnp.concatenate([value, jnp.zeros((SPAN - WIN, WIN), value.dtype)], axis=0)
-    tall = pltpu.roll(tall, shift, 0)
-    return pltpu.roll(jnp.concatenate([tall, jnp.zeros_like(tall)], axis=1), column, 1)
+    lane = lax.broadcasted_iota(jnp.int32, (8, WIN), 1)
+    sublane = lax.broadcasted_iota(jnp.int32, (8, WIN), 0)
+    zero = jnp.zeros((8, WIN), jnp.float32)
+    turned = [pltpu.roll(value[8 * j : 8 * j + 8], shift & 7, 0) for j in range(WIN // 8)]
+    placed = []
+    for j in range(SPAN // 8):
+        before = turned[j - 1] if j else zero
+        after = turned[j] if j < WIN // 8 else zero
+        row = pltpu.roll(jnp.where(sublane >= shift, after, before), column & (WIN - 1), 1)
+        placed.append(jnp.concatenate([jnp.where(lane >= column, row, 0.0), jnp.where(lane >= column, 0.0, row)], axis=1))
+    return placed
 
 
 def sum_modes(pairs):
@@ -172,8 +187,8 @@
     def deposit(slot, layer, grads):
         for part in range(2):
             value = grads[part] * lives[slot]
-            placed = spread_out(value, shifts[slot], columns[slot])
-            pad[slot, part, layer, LEAD : LEAD + SPAN // 8] = placed.reshape(SPAN // 8, 8, TILE)
+            for j, row in enumerate(spread_out(value, shifts[slot], columns[slot])):
+                pad[slot, part, layer, LEAD + j] = row
 
     def collect(layer):
         for part in range(2):
@@ -322,8 +337,8 @@
     waves = each(lambda w: right_pass(w, forward), waves)
     waves = each(lambda w: [times_conj(v, kernel()) for v in w], waves)
     waves = each(lambda w: left_pass(w, forward), waves)
+    waves = each(lambda w: right_pass(w, inverse), waves)
     sums = {chunk: spread_x(chunk, swaps[chunk]) for chunk in late}
-    waves = each(lambda w: right_pass(w, inverse), waves)
     for slot in slots:
         deposit(slot, 0, sum_modes([times_conj(waves[slot][m], probe(m)) for m in modes]))
     collect(0)

time: 43.6 us -> 43.9 us (level)
  no operation moved by 1% of the time
where the time goes in v5:
time: 43.9 us; the launch traced here: 43.8 us
  Pallas kernels  42.1 us (96%)
  local copies, waits for them, and re-layouts  0.97 us (2%)
  between operations  0.66 us (2%)
    pallas_call x1, Pallas kernels, per_device(): pl.pallas_call(fused_kernel, out_shape=pltpu.VMEM((2, LAYERS, 4, EDGE, TI...  42.1 us
    unnamed x1, local copies, waits for them, and re-layouts  0.97 us

profile of v5, /device:TPU:1, one launch (start us, length us, event | category | flops | bytes accessed | tf_op | source)
XLA Modules:
  0.0 43.8 jit_solution(5035249582099730978)
XLA Ops:
  0.7 42.1 %gradient_and_combine.1 = f32[2,2,4,64,256]{4,3,2,1,0:T(8,128)S(1)} custom-call(s32[2,2]{1,0:T(2,128)} %bitcast.9, s32[1,1]{1,0:T(1,128)S(6)} %copy.11.count_ref, f32[2,32,8,256]{3,2,1,0:T(8,128)} %bitcast.6, f32[2,32,8,256]{3,2,1,0:T(8,128)} %bitcast.7, f32[2,3,128,128]{3,2,1,0:T(8,128)} %probe_ref.1, f32[2,128,128]{2,1,0:T(8,128)} %bitcast.8, ...), custom_call_target="tpu_custom_call" | custom-call | tf_op jit(solution)/shard_map/gradient_and_combine/pallas_call | solution.py:369
  42.8 1.0 %copy.10 = f32[1,2,2,256,256]{4,3,2,1,0:T(8,128)} copy(f32[1,2,2,256,256]{4,3,2,1,0:T(8,128)S(1)} %bitcast.5) | data formatting | bytes 2097152

commit v6 on v5

--- a/solution.py
+++ b/solution.py
@@ -124,9 +124,16 @@
 
 
 def fused_kernel(
-    off_ref, count_ref, amp_ref, phase_ref, probe_ref, measured_ref, tables_ref, kernel_ref, out_ref,
-    pad, grad, pair, half, xin, block, zin, total, strips, strips_in, rows_in, send, recv,
+    off_ref, count_ref, amp_hbm, phase_hbm, probe_hbm, measured_hbm, tables_hbm, kernel_hbm, out_ref,
+    amp_ref, phase_ref, probe_ref, measured_ref, tables_ref, kernel_ref, load_sem, pad, grad, pair, half, xin, block, zin, total, strips, strips_in, rows_in, send, recv,
 ):
+    places = (
+        (amp_hbm, amp_ref), (phase_hbm, phase_ref), (probe_hbm, probe_ref), (tables_hbm, tables_ref),
+        (kernel_hbm, kernel_ref), (measured_hbm, measured_ref),
+    )
+    loads = [pltpu.make_async_copy(src, dst, load_sem.at[i]) for i, (src, dst) in enumerate(places)]
+    for load in loads:
+        load.start()
     tile, pos = lax.axis_index("tile"), lax.axis_index("pos")
     tiles = lax.axis_size("tile")
     core, z_hi, x = lax.rem(pos, 2), lax.rem(pos // 2, 2), pos // 4
@@ -166,7 +173,6 @@
     def flat(value):
         return value.reshape(4 * HIGH, TILE)
 
-    forward, inverse = tables_ref[0], tables_ref[1]
     slots = range(SLOTS)
     groups, shifts, columns = [], [], []
     lives = [(count_ref[0, 0] - slot).astype(jnp.float32) for slot in slots]
@@ -207,18 +213,26 @@
         return [stage(*items) for items in zip(*lists)]
 
     modes = range(MODES)
-    layers = []
-    for slot in slots:
-        layers.append(
-            [
-                polar(
-                    crop(amp_ref, layer, groups[slot], shifts[slot], columns[slot]),
-                    crop(phase_ref, layer, groups[slot], shifts[slot], columns[slot]),
-                )
-                for layer in range(LAYERS)
-            ]
-        )
-    waves = [[times(probe(m), layers[slot][0]) for m in modes] for slot in slots]
+    def crop_layer(layer):
+        return [
+            polar(
+                crop(amp_ref, layer, groups[slot], shifts[slot], columns[slot]),
+                crop(phase_ref, layer, groups[slot], shifts[slot], columns[slot]),
+            )
+            for slot in slots
+        ]
+
+    loads[0].wait()
+    loads[1].wait()
+    layers = [crop_layer(0)]
+    loads[2].wait()
+    loads[3].wait()
+    forward, inverse = tables_ref[0], tables_ref[1]
+    waves = [[times(probe(m), layers[0][slot]) for m in modes] for slot in slots]
+    for load in loads[4:]:
+        load.wait()
+    layers.append(crop_layer(1))
+    layers = list(zip(*layers))
     waves = each(lambda w: right_pass(w, forward), waves)
     waves = each(lambda w: left_pass(w, inverse), waves)
     waves = each(lambda w: [times(v, kernel()) for v in w], waves)
@@ -369,9 +383,16 @@
     updated = pl.pallas_call(
         fused_kernel,
         out_shape=pltpu.VMEM((2, LAYERS, 4, EDGE, TILE), f32),
-        in_specs=[smem, smem] + [vmem] * 6,
+        in_specs=[smem, smem] + [pl.BlockSpec(memory_space=pl.ANY)] * 6,
         out_specs=vmem,
         scratch_shapes=[
+            pltpu.VMEM((LAYERS, TILE // 8, 8, TILE), f32),
+            pltpu.VMEM((LAYERS, TILE // 8, 8, TILE), f32),
+            pltpu.VMEM((2, MODES, WIN, WIN), f32),
+            pltpu.VMEM((SLOTS, WIN, WIN), f32),
+            pltpu.VMEM((2, TILE, TILE), jnp.bfloat16),
+            pltpu.VMEM((2, WIN, WIN), f32),
+            pltpu.SemaphoreType.DMA((6,)),
             pltpu.VMEM((SLOTS, 2, LAYERS, 2 * LEAD + SPAN // 8, 8, TILE), f32),
             pltpu.VMEM((LAYERS, 2, 4, EDGE, TILE), f32),
             pltpu.VMEM((CHUNKS, 4, 4, HIGH, TILE), f32),

time: 43.9 us -> 42.7 us (0.973)
  Pallas kernels: 42.1 us -> 40.9 us
    pallas_call x1, Pallas kernels: 42.1 us -> 40.9 us  [per_device(): pl.pallas_call(fused_kernel, out_shape=pltpu.VMEM((2, LAYERS, 4, EDGE, TI...]
where the time goes in v6:
time: 42.7 us; the launch traced here: 42.5 us
  Pallas kernels  40.9 us (96%)
  local copies, waits for them, and re-layouts  0.97 us (2%)
  between operations  0.66 us (2%)
    pallas_call x1, Pallas kernels, per_device(): pl.pallas_call(fused_kernel, out_shape=pltpu.VMEM((2, LAYERS, 4, EDGE, TI...  40.9 us
    unnamed x1, local copies, waits for them, and re-layouts  0.97 us

profile of v6, /device:TPU:1, one launch (start us, length us, event | category | flops | bytes accessed | tf_op | source)
XLA Modules:
  0.0 42.5 jit_solution(16527965479711367217)
XLA Ops:
  0.7 40.9 %gradient_and_combine.1 = f32[2,2,4,64,256]{4,3,2,1,0:T(8,128)S(1)} custom-call(s32[2,2]{1,0:T(2,128)} %bitcast.9, s32[1,1]{1,0:T(1,128)S(6)} %copy.11.count_ref, f32[2,32,8,256]{3,2,1,0:T(8,128)} %bitcast.6, f32[2,32,8,256]{3,2,1,0:T(8,128)} %bitcast.7, f32[2,3,128,128]{3,2,1,0:T(8,128)} %probe_hbm.1, f32[2,128,128]{2,1,0:T(8,128)} %bitcast.8, ...), custom_call_target="tpu_custom_call" | custom-call | tf_op jit(solution)/shard_map/gradient_and_combine/pallas_call | solution.py:383
  41.6 1.0 %copy.10 = f32[1,2,2,256,256]{4,3,2,1,0:T(8,128)} copy(f32[1,2,2,256,256]{4,3,2,1,0:T(8,128)S(1)} %bitcast.5) | data formatting | bytes 2097152

commit v7 on v6

--- a/solution.py
+++ b/solution.py
@@ -145,13 +145,14 @@
 
     sibling = at(0, x, z_hi, 1 - core)
     along_x = {step: at(0, xs[step], z_hi, core) for step in (1, 2, 3)}
+    crossed = {step: at(0, xs[step], z_hi, 1 - core) for step in (1, 2, 3)}
     across = at(0, x, 1 - z_hi, core)
     after = at(1, x, jnp.where(z_lo == 3, 1 - z_hi, z_hi), core)
     before = at(-1, x, jnp.where(z_lo == 0, 1 - z_hi, z_hi), core)
     below = at(4, x, z_hi, core)
     above = at(-4, x, z_hi, core)
 
-    partners = (sibling, along_x[1], along_x[3], along_x[2], across, after, before, below, above)
+    partners = (sibling, along_x[1], along_x[3], along_x[2], across, after, before, below, above) + tuple(crossed.values())
     barrier = pltpu.get_barrier_semaphore()
     for partner in partners:
         pl.semaphore_signal(barrier, inc=1, device_id=partner, device_id_type=MESH)
@@ -224,14 +225,11 @@
 
     loads[0].wait()
     loads[1].wait()
-    layers = [crop_layer(0)]
-    loads[2].wait()
-    loads[3].wait()
+    layers = [crop_layer(layer) for layer in range(LAYERS)]
+    for load in loads[2:]:
+        load.wait()
     forward, inverse = tables_ref[0], tables_ref[1]
     waves = [[times(probe(m), layers[0][slot]) for m in modes] for slot in slots]
-    for load in loads[4:]:
-        load.wait()
-    layers.append(crop_layer(1))
     layers = list(zip(*layers))
     waves = each(lambda w: right_pass(w, forward), waves)
     waves = each(lambda w: left_pass(w, inverse), waves)
@@ -333,11 +331,16 @@
         combined = flat(total[chunk]) + jnp.concatenate([left, right], axis=1) + ends
         out_ref[x // 2, layer, :, rows_of(x, core, sub), :] = (base - STEP * combined).reshape(4, HIGH, TILE)
         remote = [(step, share(chunk, 11 + step, 0, along_x[step])) for step in (2, 1, 3)]
-        return remote, [share(chunk, 15, 0, sibling)]
+        local = [share(chunk, 15, 0, sibling)]
+        if chunk == SUBS - 1:
+            local += [share(chunk, 15 + step, 0, crossed[step]) for step in (2, 1, 3)]
+        return remote, local
 
     def relay(chunk, remote, local):
         for step, copy in remote:
             copy.wait_recv()
+            if chunk == SUBS - 1:
+                continue
             local.append(share(chunk, 15 + step, 4 - step, sibling))
         return local
 

time: 42.7 us -> 42.5 us (level)
  no operation moved by 1% of the time
where the time goes in v7:
time: 42.5 us; the launch traced here: 42.4 us
  Pallas kernels  40.8 us (96%)
  local copies, waits for them, and re-layouts  0.97 us (2%)
  between operations  0.66 us (2%)
    pallas_call x1, Pallas kernels, per_device(): pl.pallas_call(fused_kernel, out_shape=pltpu.VMEM((2, LAYERS, 4, EDGE, TI...  40.8 us
    unnamed x1, local copies, waits for them, and re-layouts  0.97 us

profile of v7, /device:TPU:1, one launch (start us, length us, event | category | flops | bytes accessed | tf_op | source)
XLA Modules:
  0.0 42.4 jit_solution(5131325705819246611)
XLA Ops:
  0.7 40.8 %gradient_and_combine.1 = f32[2,2,4,64,256]{4,3,2,1,0:T(8,128)S(1)} custom-call(s32[2,2]{1,0:T(2,128)} %bitcast.9, s32[1,1]{1,0:T(1,128)S(6)} %copy.11.count_ref, f32[2,32,8,256]{3,2,1,0:T(8,128)} %bitcast.6, f32[2,32,8,256]{3,2,1,0:T(8,128)} %bitcast.7, f32[2,3,128,128]{3,2,1,0:T(8,128)} %probe_hbm.1, f32[2,128,128]{2,1,0:T(8,128)} %bitcast.8, ...), custom_call_target="tpu_custom_call" | custom-call | tf_op jit(solution)/shard_map/gradient_and_combine/pallas_call | solution.py:386
  41.4 1.0 %copy.10 = f32[1,2,2,256,256]{4,3,2,1,0:T(8,128)} copy(f32[1,2,2,256,256]{4,3,2,1,0:T(8,128)S(1)} %bitcast.5) | data formatting | bytes 2097152
